TPU v7x, 256 devices: a whole 4x4x8 slice. The times are simulated.
256 devices in a mesh: tgt: 64 (over x, z, core), sec: 4 (over y).
Axes of the slice: x: 4, y: 4, z: 8, core: 2. Of those that a mesh axis runs over, the one named last changes fastest.
Arguments:
- queries: bfloat16 [16384, 4096], P('tgt', 'sec'), may hold values from -210 to 210
- key_values: bfloat16 [2, 16384, 4096], P(None, 'tgt', 'sec'), may hold values from -6.06 to 6.06
- grad_out: bfloat16 [16384, 4096], P('tgt', 'sec'), may hold values from -192 to 192
- block_ids: int32 [128, 4], P('tgt'), may hold values from 0 to 127, as said below
- block_count: int32 [128], P('tgt'), may hold values from 1 to 4, as said below
- kv_weight: bfloat16 [2, 4096, 4096], P(None, 'tgt', 'sec'), may hold values from -0.0625 to 0.0625
Outputs:
- grad_queries: bfloat16 [16384, 4096], P('tgt', 'sec')
- grad_memory: bfloat16 [16384, 4096], P('tgt', 'sec')
Inputs may be any that keep to these rules, and one draw needn't show every extreme that they name: `block_ids`: target block i, which lies in the rows of index t = i // 2 of tgt, lists only source blocks in the rows of indices t - 1, t and t + 1; its first entry is block i itself; its live entries are distinct; entries past its count repeat block i. `block_count`: every eighth block, starting at block 3, has all slots live.
All inputs are finite; a program needn't handle non-finite values.
Results may differ from a plain program's by a relative error of at most 0.013.
Values may be sent and summed in bfloat16 or wider, within the bound.
A program may use at most 128 MiB of HBM per device.

v0:
```python
import jax
import jax.numpy as jnp
from jax import lax
from jax.sharding import PartitionSpec as P

HEAD_DIM = 64
BLOCK = 128
SLOTS = 4


def from_behind(block, axis, distance):
    devices = range(lax.axis_size(axis))
    route = [(i - distance, i) for i in devices if i - distance in devices]
    return lax.ppermute(block, axis, route)


def with_halo(block, sides, width):
    for axis, dim in sides:
        count = lax.axis_size(axis)
        forward = [(i, i + 1) for i in range(count - 1)]
        backward = [(target, source) for source, target in forward]
        low = lax.ppermute(
            lax.slice_in_dim(block, block.shape[dim] - width, None, axis=dim), axis, forward
        )
        high = lax.ppermute(lax.slice_in_dim(block, 0, width, axis=dim), axis, backward)
        block = jnp.concatenate([low, block, high], axis=dim)
    return block


def send_back(part_grads, offset):
    return from_behind(part_grads.astype(jnp.bfloat16), "tgt", offset).astype(part_grads.dtype)


def per_device(queries, key_values, grad_out, block_ids, block_count, kv_weight):
    rows_here = queries.shape[0]
    width_here = queries.shape[1]
    heads_here = width_here // HEAD_DIM
    blocks_here = rows_here // BLOCK
    device_pos = lax.axis_index("tgt")
    extended = with_halo(key_values, (("tgt", 1),), rows_here)
    local_ids = block_ids - (device_pos - 1) * blocks_here
    ext_blocks = extended.reshape(2, 3 * blocks_here, BLOCK, width_here)
    ext_range = jnp.arange(3 * blocks_here)

    def block_step(carry, inputs):
        query_block, upstream_block, listed, count = inputs
        picked = ext_blocks[:, listed]
        key_rows = picked[0].reshape(SLOTS * BLOCK, heads_here, HEAD_DIM)
        value_rows = picked[1].reshape(SLOTS * BLOCK, heads_here, HEAD_DIM)
        query_rows = query_block.reshape(BLOCK, heads_here, HEAD_DIM)
        upstream = upstream_block.reshape(BLOCK, heads_here, HEAD_DIM)
        slot_live = jnp.arange(SLOTS) < count
        key_live = jnp.repeat(slot_live, BLOCK)
        scores = 0.125 * jnp.einsum(
            "qhd,khd->hqk", query_rows, key_rows, preferred_element_type=jnp.float32
        )
        scores = jnp.where(key_live[None, None, :], scores, -jnp.inf)
        row_max = jnp.max(scores, axis=-1, keepdims=True)
        expo = jnp.exp(scores - row_max)
        probs = expo / jnp.sum(expo, axis=-1, keepdims=True)
        probs_half = probs.astype(jnp.bfloat16)
        attended = jnp.einsum(
            "hqk,khd->qhd", probs_half, value_rows, preferred_element_type=jnp.float32
        )
        delta = jnp.sum(upstream.astype(jnp.float32) * attended, axis=-1)
        grad_probs = jnp.einsum(
            "qhd,khd->hqk", upstream, value_rows, preferred_element_type=jnp.float32
        )
        grad_scores = probs * (grad_probs - jnp.transpose(delta)[:, :, None])
        grad_half = grad_scores.astype(jnp.bfloat16)
        grad_query = 0.125 * jnp.einsum(
            "hqk,khd->qhd", grad_half, key_rows, preferred_element_type=jnp.float32
        )
        grad_key = 0.125 * jnp.einsum(
            "hqk,qhd->khd", grad_half, query_rows, preferred_element_type=jnp.float32
        )
        grad_value = jnp.einsum(
            "hqk,qhd->khd", probs_half, upstream, preferred_element_type=jnp.float32
        )
        pair_grads = jnp.stack([grad_key, grad_value]).reshape(2, SLOTS, BLOCK, width_here)
        targets = ((listed[:, None] == ext_range[None, :]) & slot_live[:, None]).astype(jnp.float32)
        carry = carry + jnp.einsum(
            "sj,csrx->cjrx", targets, pair_grads, precision=lax.Precision.HIGHEST
        )
        return (carry, grad_query.reshape(BLOCK, width_here).astype(jnp.bfloat16))

    start = jnp.zeros((2, 3 * blocks_here, BLOCK, width_here), jnp.float32)
    inputs = (
        queries.reshape(blocks_here, BLOCK, width_here),
        grad_out.reshape(blocks_here, BLOCK, width_here),
        local_ids,
        block_count,
    )
    spread_blocks, query_blocks = lax.scan(block_step, start, inputs)
    spread = spread_blocks.reshape(2, 3 * rows_here, width_here)
    own_grads = spread[:, rows_here : 2 * rows_here]
    own_grads = (
        own_grads + send_back(spread[:, :rows_here], -1) + send_back(spread[:, 2 * rows_here :], 1)
    )
    grads_half = own_grads.astype(jnp.bfloat16)
    partial_memory = jnp.einsum(
        "crx,cnx->rn",
        grads_half,
        lax.all_gather(kv_weight, "tgt", axis=1, tiled=True),
        preferred_element_type=jnp.float32,
    )
    total_memory = lax.psum(partial_memory.astype(jnp.bfloat16), "sec").astype(jnp.float32)
    columns = total_memory.shape[1] // lax.axis_size("sec")
    grad_memory = lax.dynamic_slice_in_dim(
        total_memory, lax.axis_index("sec") * columns, columns, 1
    ).astype(jnp.bfloat16)
    grad_queries = query_blocks.reshape(rows_here, width_here)
    return (grad_queries, grad_memory)


def solution(mesh):
    return jax.shard_map(
        per_device,
        mesh=mesh,
        in_specs=(
            P("tgt", "sec"),
            P(None, "tgt", "sec"),
            P("tgt", "sec"),
            P("tgt", None),
            P("tgt"),
            P(None, "tgt", "sec"),
        ),
        out_specs=(P("tgt", "sec"), P("tgt", "sec")),
        check_vma=False,
    )
```

profile of v0, /device:TPU:1, one launch (start us, length us, event | category | flops | bytes accessed | tf_op | source)
XLA Modules:
  0.0 269.9 jit_solution(8418963483960269523)
XLA Ops:
  7.9 4.9 %collective-permute-start = (bf16[2,256,1024]{2,1,0:T(8,128)(2,1)}, bf16[2,256,1024]{2,1,0:T(8,128)(2,1)S(1)}, u32[]{:S(2)}, u32[]{:S(2)}) collective-permute-start(bf16[2,256,1024]{2,1,0:T(8,128)(2,1)} %param.9), channel_id=1, source_target_pairs={{0,4},{4,8},{8,12},{12,16},{16,20},{20,24},{24,28},{28,32},{32,36}... | collective-permute-start | bytes 3145736 | tf_op jit(solution)/shard_map/ppermute | solution.py:22
  12.9 1.9 collective-permute-start.1
  15.5 9.4 %collective-permute-done = bf16[2,256,1024]{2,1,0:T(8,128)(2,1)S(1)} collective-permute-done((bf16[2,256,1024]{2,1,0:T(8,128)(2,1)}, bf16[2,256,1024]{2,1,0:T(8,128)(2,1)S(1)}, u32[]{:S(2)}, u32[]{:S(2)}) %collective-permute-start) | collective-permute-done | bytes 1048608 | tf_op jit(solution)/shard_map/ppermute | solution.py:22
  24.9 4.3 %collective-permute-done.1 = bf16[2,256,1024]{2,1,0:T(8,128)(2,1)S(1)} collective-permute-done((bf16[2,256,1024]{2,1,0:T(8,128)(2,1)}, bf16[2,256,1024]{2,1,0:T(8,128)(2,1)S(1)}, u32[]{:S(2)}, u32[]{:S(2)}) %collective-permute-start.1) | collective-permute-done | bytes 1048608 | tf_op jit(solution)/shard_map/ppermute | solution.py:25
  29.2 2.8 %pad_maximum_fusion = bf16[2,768,1024]{2,1,0:T(8,128)(2,1)} fusion(bf16[2,256,1024]{2,1,0:T(8,128)(2,1)S(1)} %collective-permute-done.1, bf16[2,256,1024]{2,1,0:T(8,128)(2,1)} %param.9, bf16[2,256,1024]{2,1,0:T(8,128)(2,1)S(1)} %collective-permute-done), kind=kLoop, calls=%fused_computation.45 | loop fusion | flops 9437184 | bytes 6291456 | tf_op jit(solution)/shard_map/concatenate | solution.py:26
  32.0 116.6 %while.13 = (s32[]{:T(128)}, f32[2,6,128,1024]{3,1,2,0:T(8,128)}, bf16[2,128,1024]{2,1,0:T(8,128)(2,1)}, bf16[2,128,1024]{2,1,0:T(8,128)(2,1)}, s32[2]{0:T(128)S...) while((s32[]{:T(128)}, f32[2,6,128,1024]{3,1,2,0:T(8,128)}, ...), condition=%wide.region_4.5_spmd.clone, body=%wide.region_0.4_spmd.clone.sunk | while | flops 896663104 | bytes 128497184 | solution.py:94
  32.1 2.6 gather_fusion
  34.7 1.2 fusion.87
  39.5 3.4 %fusion.88 = (f32[16,128]{1,0:T(8,128)S(1)}, f32[16,128,512]{2,1,0:T(8,128)}) fusion(pred[512]{0:T(512)(128)(4,1)S(1)} %broadcast_bitcast_fusion.2, bf16[128,16,64]{0,2,1:T(8,128)(2,1)S(1)} %bitcast.125, bf16[512,16,64]{0,2,1:T(8,128)(2,1)S(1)} %squeeze.23), kind=kOutput, calls=%fused_computation.53.clone.1 | convolution fusion | flops 138412544 | bytes 5513728 | tf_op jit(solution)/shard_map/while/body/eval_jaxpr/sub | solution.py:59
  42.8 2.6 fusion.89
  45.4 2.4 copy.37
  47.8 2.3 squeeze.24
  51.2 2.1 fusion.90
  53.4 2.8 %multiply_convert_fusion.2 = bf16[16,128,512]{2,1,0:T(8,128)(2,1)S(1)} fusion(bf16[128,16,64]{0,2,1:T(8,128)(2,1)S(1)} %bitcast.123, bf16[512,16,64]{0,2,1:T(8,128)(2,1)S(1)} %copy-done.3, f32[16,128]{1,0:T(8,128)S(1)} %bitcast.131, f32[16,128,512]{2,1,0:T(8,128)} %get-tuple-element.171, f32[16,128]{1,0:T(8,128)S(1)} %get-tuple-element.172), kind=kOutput, calls=%fused_computation.8.clone.1 | convolution fusion | flops 138412032 | bytes 7618560 | tf_op jit(solution)/shard_map/while/body/eval_jaxpr/qhd,khd->hqk/dot_general | solution.py:66
  56.2 1.4 copy-done.1
  57.6 1.8 multiply_bitcast_fusion.2
  59.4 2.9 %stack.15 = f32[1,4,128,1024]{2,1,3,0:T(4,128)} reshape(f32[512,16,64]{0,2,1:T(8,128)} %multiply_bitcast_fusion.2) | data formatting | bytes 4194304 | tf_op jit(solution)/shard_map/while/body/eval_jaxpr/stack | solution.py:80
  62.3 3.9 %copy.38 = f32[1,4,128,1024]{3,1,2,0:T(4,128)} copy(f32[1,4,128,1024]{2,1,3,0:T(4,128)} %stack.15) | data formatting | bytes 4194304 | tf_op jit(solution)/shard_map/while/body/eval_jaxpr/stack | solution.py:80
  66.2 1.7 convolution_bitcast_fusion.4
  67.9 2.9 %stack.14 = f32[1,4,128,1024]{2,1,3,0:T(4,128)} reshape(f32[512,16,64]{0,2,1:T(8,128)} %convolution_bitcast_fusion.4) | data formatting | bytes 4194304 | tf_op jit(solution)/shard_map/while/body/eval_jaxpr/stack | solution.py:80
  70.8 4.1 %copy.36 = f32[1,4,128,1024]{3,1,2,0:T(4,128)} copy(f32[1,4,128,1024]{2,1,3,0:T(4,128)} %stack.14) | data formatting | bytes 4194304 | tf_op jit(solution)/shard_map/while/body/eval_jaxpr/stack | solution.py:80
  74.9 12.2 %bitcast_add_fusion.2 = f32[2,6,128,1024]{3,1,2,0:T(8,128)} fusion(f32[2,6,128,1024]{3,1,2,0:T(8,128)} %get-tuple-element.185, pred[]{:T(512)S(6)} %compare.3, f32[1,4,128,1024]{3,1,2,0:T(4,128)} %copy.36, f32[1,4,128,1024]{3,1,2,0:T(4,128)S(1)} %copy-done, s32[4]{0:T(128)S(1)} %fusion.91, pred[4]{0:T(512)(128)(4,1)S(1)} %iota_compare_fusion.3), kind=kOutput, calls=%fused_computation.3.clone.1 | convolution fusion | flops 79691824 | bytes 16777236 | tf_op jit(solution)/shard_map/while/body/eval_jaxpr/sj,csrx->cjrx/dot_general | solution.py:82
  89.1 2.7 %gather_fusion = bf16[4,2,128,1024]{3,2,1,0:T(8,128)(2,1)S(1)} fusion(bf16[2,6,128,1024]{3,2,1,0:T(8,128)(2,1)} %get-tuple-element.200, s32[1024]{0:T(1024)S(1)} %pad_clamp_fusion.2), kind=kCustom, calls=%fused_computation.clone.clone.1 | custom fusion | bytes 4194320 | tf_op jit(solution)/shard_map/while/body/eval_jaxpr/gather | solution.py:47
  91.8 1.2 fusion.87
  96.6 3.4 %fusion.88 = (f32[16,128]{1,0:T(8,128)S(1)}, f32[16,128,512]{2,1,0:T(8,128)}) fusion(pred[512]{0:T(512)(128)(4,1)S(1)} %broadcast_bitcast_fusion.2, bf16[128,16,64]{0,2,1:T(8,128)(2,1)S(1)} %bitcast.125, bf16[512,16,64]{0,2,1:T(8,128)(2,1)S(1)} %squeeze.23), kind=kOutput, calls=%fused_computation.53.clone.1 | convolution fusion | flops 138412544 | bytes 5513728 | tf_op jit(solution)/shard_map/while/body/eval_jaxpr/sub | solution.py:59
  100.0 2.6 fusion.89
  102.6 2.4 copy.37
  105.1 2.3 squeeze.24
  107.3 1.1 copy.33
  108.4 2.1 fusion.90
  110.6 2.9 %multiply_convert_fusion.2 = bf16[16,128,512]{2,1,0:T(8,128)(2,1)S(1)} fusion(bf16[128,16,64]{0,2,1:T(8,128)(2,1)S(1)} %bitcast.123, bf16[512,16,64]{0,2,1:T(8,128)(2,1)S(1)} %copy-done.3, f32[16,128]{1,0:T(8,128)S(1)} %bitcast.131, f32[16,128,512]{2,1,0:T(8,128)} %get-tuple-element.171, f32[16,128]{1,0:T(8,128)S(1)} %get-tuple-element.172), kind=kOutput, calls=%fused_computation.8.clone.1 | convolution fusion | flops 138412032 | bytes 7618560 | tf_op jit(solution)/shard_map/while/body/eval_jaxpr/qhd,khd->hqk/dot_general | solution.py:66
  113.6 1.4 copy-done.1
  115.0 1.8 multiply_bitcast_fusion.2
  116.7 2.9 %stack.15 = f32[1,4,128,1024]{2,1,3,0:T(4,128)} reshape(f32[512,16,64]{0,2,1:T(8,128)} %multiply_bitcast_fusion.2) | data formatting | bytes 4194304 | tf_op jit(solution)/shard_map/while/body/eval_jaxpr/stack | solution.py:80
  119.6 3.9 %copy.38 = f32[1,4,128,1024]{3,1,2,0:T(4,128)} copy(f32[1,4,128,1024]{2,1,3,0:T(4,128)} %stack.15) | data formatting | bytes 4194304 | tf_op jit(solution)/shard_map/while/body/eval_jaxpr/stack | solution.py:80
  123.5 1.7 convolution_bitcast_fusion.4
  125.3 2.9 %stack.14 = f32[1,4,128,1024]{2,1,3,0:T(4,128)} reshape(f32[512,16,64]{0,2,1:T(8,128)} %convolution_bitcast_fusion.4) | data formatting | bytes 4194304 | tf_op jit(solution)/shard_map/while/body/eval_jaxpr/stack | solution.py:80
  128.2 4.1 %copy.36 = f32[1,4,128,1024]{3,1,2,0:T(4,128)} copy(f32[1,4,128,1024]{2,1,3,0:T(4,128)} %stack.14) | data formatting | bytes 4194304 | tf_op jit(solution)/shard_map/while/body/eval_jaxpr/stack | solution.py:80
  132.3 14.5 %bitcast_add_fusion.2 = f32[2,6,128,1024]{3,1,2,0:T(8,128)} fusion(f32[2,6,128,1024]{3,1,2,0:T(8,128)} %get-tuple-element.185, pred[]{:T(512)S(6)} %compare.3, f32[1,4,128,1024]{3,1,2,0:T(4,128)} %copy.36, f32[1,4,128,1024]{3,1,2,0:T(4,128)S(1)} %copy-done, s32[4]{0:T(128)S(1)} %fusion.91, pred[4]{0:T(512)(128)(4,1)S(1)} %iota_compare_fusion.3), kind=kOutput, calls=%fused_computation.3.clone.1 | convolution fusion | flops 79691824 | bytes 16777236 | tf_op jit(solution)/shard_map/while/body/eval_jaxpr/sj,csrx->cjrx/dot_general | solution.py:82
  148.6 7.0 %copy.20 = f32[2,6,128,1024]{3,2,1,0:T(8,128)S(1)} copy(f32[2,6,128,1024]{3,1,2,0:T(8,128)} %get-tuple-element.51) | data formatting | bytes 12582912 | tf_op jit(solution)/shard_map/while | solution.py:94
  156.1 2.2 copy-done.6
  158.5 1.9 collective-permute-start.2
  160.4 3.6 %collective-permute-start.3 = (bf16[2,256,1024]{2,1,0:T(8,128)(2,1)S(1)}, bf16[2,256,1024]{2,1,0:T(8,128)(2,1)S(1)}, u32[]{:S(2)}, u32[]{:S(2)}) collective-permute-start(bf16[2,256,1024]{2,1,0:T(8,128)(2,1)S(1)} %get-tuple-element.112), channel_id=1, source_target_pairs={{0,4},{4,8},{8,12},{12,16},{16,20},{20,24},{24,28},{28,32},{32,36}... | collective-permute-start | bytes 3145736 | tf_op jit(solution)/shard_map/ppermute | solution.py:14
  164.0 10.5 %collective-permute-done.2 = bf16[2,256,1024]{2,1,0:T(8,128)(2,1)S(1)} collective-permute-done((bf16[2,256,1024]{2,1,0:T(8,128)(2,1)S(1)}, bf16[2,256,1024]{2,1,0:T(8,128)(2,1)S(1)}, u32[]{:S(2)}, u32[]{:S(2)}) %collective-permute-start.2) | collective-permute-done | bytes 1048608 | tf_op jit(solution)/shard_map/ppermute | solution.py:14
  174.6 1.2 collective-permute-done.3
  175.8 12.3 %fusion.29 = bf16[256,4096]{1,0:T(8,128)(2,1)} fusion(bf16[2,4096,1024]{2,1,0:T(8,128)(2,1)} %all-gather.2.cloned.1.call-done, f32[2,768,1024]{2,1,0:T(8,128)} %bitcast.128, bf16[2,256,1024]{2,1,0:T(8,128)(2,1)S(1)} %collective-permute-done.3, bf16[2,256,1024]{2,1,0:T(8,128)(2,1)S(1)} %collective-permute-done.2), kind=kOutput, calls=%fused_computation.44 | convolution fusion | flops 4298637312 | bytes 23068672 | tf_op jit(solution)/shard_map/crx,cnx->rn/dot_general | solution.py:101
  188.1 73.1 %all-reduce.2.cloned.1.call-done = bf16[256,4096]{1,0:T(8,128)(2,1)} async-done(((bf16[256,4096]{1,0:T(8,128)(2,1)}), bf16[256,4096]{1,0:T(8,128)(2,1)}) %all-reduce.2.cloned.1.call-update) | async-done | bytes 2097168 | tf_op jit(solution)/shard_map/psum | solution.py:107
  261.1 1.9 convert_convert_fusion
  (78 shorter events, 14.1 us)
Async XLA Ops:
  7.2 168.6 %all-gather.2.cloned.1.call-start = ((), (), s32[]{:S(2)}) async-start(), calls=%async_computation | async-start | bytes 17039360 | tf_op jit(solution)/shard_map/all_gather | solution.py:104
  7.9 253.3 %all-reduce.2.cloned.1.call-start = ((), (), s32[]{:S(2)}) async-start(), calls=%async_computation.1 | async-start | bytes 4194304 | tf_op jit(solution)/shard_map/psum | solution.py:107
  7.9 17.0 %collective-permute-start = (bf16[2,256,1024]{2,1,0:T(8,128)(2,1)}, bf16[2,256,1024]{2,1,0:T(8,128)(2,1)S(1)}, u32[]{:S(2)}, u32[]{:S(2)}) collective-permute-start(bf16[2,256,1024]{2,1,0:T(8,128)(2,1)} %param.9), channel_id=1, source_target_pairs={{0,4},{4,8},{8,12},{12,16},{16,20},{20,24},{24,28},{28,32},{32,36}... | collective-permute-start | bytes 3145736 | tf_op jit(solution)/shard_map/ppermute | solution.py:22
  12.9 16.3 %collective-permute-start.1 = (bf16[2,256,1024]{2,1,0:T(8,128)(2,1)}, bf16[2,256,1024]{2,1,0:T(8,128)(2,1)S(1)}, u32[]{:S(2)}, u32[]{:S(2)}) collective-permute-start(bf16[2,256,1024]{2,1,0:T(8,128)(2,1)} %param.9), channel_id=1, source_target_pairs={{4,0},{8,4},{12,8},{16,12},{20,16},{24,20},{28,24},{32,28},{36,32}... | collective-permute-start | bytes 3145736 | tf_op jit(solution)/shard_map/ppermute | solution.py:25
  15.5 16.5 %copy-start.11 = (s32[2]{0:T(128)S(1)}, s32[2]{0:T(128)}, u32[]{:S(2)}) copy-start(s32[2]{0:T(128)} %param.12) | copy-start | bytes 28
  35.9 1.2 copy-start.7
  35.9 1.2 copy-start.8
  38.1 4.8 %copy-start.4 = (bf16[1,128,1024]{1,2,0:T(8,128)(2,1)}, bf16[1,128,1024]{1,2,0:T(8,128)(2,1)S(1)}, u32[]{:S(2)}) copy-start(bf16[1,128,1024]{1,2,0:T(8,128)(2,1)S(1)} %copy.34) | copy-start | bytes 786436 | tf_op jit(solution)/shard_map/while
  51.2 2.2 copy-start.3
  53.4 4.2 %copy-start.5 = (bf16[1,128,1024]{1,2,0:T(8,128)(2,1)S(1)}, bf16[1,128,1024]{1,2,0:T(8,128)(2,1)}, u32[]{:S(2)}) copy-start(bf16[1,128,1024]{1,2,0:T(8,128)(2,1)} %copy-done.4) | copy-start | bytes 786436 | tf_op jit(solution)/shard_map/while
  56.2 1.4 copy-start.1
  70.8 4.1 %copy-start = (f32[1,4,128,1024]{3,1,2,0:T(4,128)S(1)}, f32[1,4,128,1024]{3,1,2,0:T(4,128)}, u32[]{:S(2)}) copy-start(f32[1,4,128,1024]{3,1,2,0:T(4,128)} %copy.38) | copy-start | bytes 6291460 | tf_op jit(solution)/shard_map/while
  74.9 12.2 %copy-start.2 = (bf16[16,128,512]{2,1,0:T(8,128)(2,1)S(1)}, bf16[16,128,512]{2,1,0:T(8,128)(2,1)}, u32[]{:S(2)}) copy-start(bf16[16,128,512]{2,1,0:T(8,128)(2,1)} %copy-done.1) | copy-start | bytes 6291460 | tf_op jit(solution)/shard_map/while
  87.1 1.2 copy-start.9
  88.3 0.8 copy-start.10
  93.1 1.2 copy-start.7
  93.1 1.2 copy-start.8
  95.2 4.8 %copy-start.4 = (bf16[1,128,1024]{1,2,0:T(8,128)(2,1)}, bf16[1,128,1024]{1,2,0:T(8,128)(2,1)S(1)}, u32[]{:S(2)}) copy-start(bf16[1,128,1024]{1,2,0:T(8,128)(2,1)S(1)} %copy.34) | copy-start | bytes 786436 | tf_op jit(solution)/shard_map/while
  108.4 2.2 copy-start.3
  110.6 4.3 %copy-start.5 = (bf16[1,128,1024]{1,2,0:T(8,128)(2,1)S(1)}, bf16[1,128,1024]{1,2,0:T(8,128)(2,1)}, u32[]{:S(2)}) copy-start(bf16[1,128,1024]{1,2,0:T(8,128)(2,1)} %copy-done.4) | copy-start | bytes 786436 | tf_op jit(solution)/shard_map/while
  113.6 1.4 copy-start.1
  128.2 4.1 %copy-start = (f32[1,4,128,1024]{3,1,2,0:T(4,128)S(1)}, f32[1,4,128,1024]{3,1,2,0:T(4,128)}, u32[]{:S(2)}) copy-start(f32[1,4,128,1024]{3,1,2,0:T(4,128)} %copy.38) | copy-start | bytes 6291460 | tf_op jit(solution)/shard_map/while
  132.2 14.5 %copy-start.2 = (bf16[16,128,512]{2,1,0:T(8,128)(2,1)S(1)}, bf16[16,128,512]{2,1,0:T(8,128)(2,1)}, u32[]{:S(2)}) copy-start(bf16[16,128,512]{2,1,0:T(8,128)(2,1)} %copy-done.1) | copy-start | bytes 6291460 | tf_op jit(solution)/shard_map/while
  146.7 1.0 copy-start.9
  147.8 0.8 copy-start.10
  155.6 2.7 copy-start.6
  158.5 16.1 %collective-permute-start.2 = (bf16[2,256,1024]{2,1,0:T(8,128)(2,1)S(1)}, bf16[2,256,1024]{2,1,0:T(8,128)(2,1)S(1)}, u32[]{:S(2)}, u32[]{:S(2)}) collective-permute-start(bf16[2,256,1024]{2,1,0:T(8,128)(2,1)S(1)} %get-tuple-element.111), channel_id=1, source_target_pairs={{4,0},{8,4},{12,8},{16,12},{20,16},{24,20},{28,24},{32,28},{36,32}... | collective-permute-start | bytes 3145736 | tf_op jit(solution)/shard_map/ppermute | solution.py:14
  160.4 15.4 %collective-permute-start.3 = (bf16[2,256,1024]{2,1,0:T(8,128)(2,1)S(1)}, bf16[2,256,1024]{2,1,0:T(8,128)(2,1)S(1)}, u32[]{:S(2)}, u32[]{:S(2)}) collective-permute-start(bf16[2,256,1024]{2,1,0:T(8,128)(2,1)S(1)} %get-tuple-element.112), channel_id=1, source_target_pairs={{0,4},{4,8},{8,12},{12,16},{16,20},{20,24},{24,28},{28,32},{32,36}... | collective-permute-start | bytes 3145736 | tf_op jit(solution)/shard_map/ppermute | solution.py:14
Sparse Core Ops, SparseCore 0:
  10.8 104.2 all-gather.1
  188.2 72.9 all-reduce.1
where the time goes:
time: 271 us; the launch traced here: 270 us
  waiting for transfers between devices  99.2 us (37%)
  local copies, waits for them, and re-layouts  67 us (25%)
  matrix products  64.3 us (24%)
  between operations  14.1 us (5%)
  starting transfers between devices  12.5 us (5%)
  other arithmetic  12.4 us (5%)
    psum x1, waiting for transfers between devices, per_device(): lax.psum(partial_memory.astype(jnp.bfloat16), 'sec').astype(jnp.float32)  73.1 us
    another operation x8, local copies, waits for them, and re-layouts, block_step(): jnp.stack([grad_key, grad_value]).reshape(2, SLOTS, BLOCK, width_here)  27.6 us
    dot_general x2, matrix products, block_step(): jnp.einsum('sj,csrx->cjrx', targets, pair_grads, precision=lax.Precision....  26.7 us
    dot_general x1, matrix products, per_device(): jnp.einsum('crx,cnx->rn', grads_half, lax.all_gather(kv_weight, 'tgt', ax...  12.3 us
    ppermute x2, waiting for transfers between devices, from_behind(): return lax.ppermute(block, axis, route)  11.7 us
    ppermute x1, waiting for transfers between devices, with_halo(): lax.ppermute(lax.slice_in_dim(block, block.shape[dim] - width, None, axis...  9.39 us
    slice x4, local copies, waits for them, and re-layouts, block_step(): value_rows = picked[1].reshape(SLOTS * BLOCK, heads_here, HEAD_DIM)  7.31 us
    while x1, local copies, waits for them, and re-layouts, per_device(): spread_blocks, query_blocks = lax.scan(block_step, start, inputs)  7.02 us
  transfers between devices with their start and end apart: 6, of which 5 were waited for; matrix products, arithmetic and copies ran while one was open for 45% of the time, Pallas kernels for 0%

commit v1 on v0

--- a/solution.py
+++ b/solution.py
@@ -104,7 +104,9 @@
         lax.all_gather(kv_weight, "tgt", axis=1, tiled=True),
         preferred_element_type=jnp.float32,
     )
-    total_memory = lax.psum(partial_memory.astype(jnp.bfloat16), "sec").astype(jnp.float32)
+    total_memory = jnp.sum(
+        lax.all_gather(partial_memory.astype(jnp.bfloat16), "sec"), axis=0
+    ).astype(jnp.float32)
     columns = total_memory.shape[1] // lax.axis_size("sec")
     grad_memory = lax.dynamic_slice_in_dim(
         total_memory, lax.axis_index("sec") * columns, columns, 1

time: 271 us -> 297 us (1.096)
  waiting for transfers between devices: 99.2 us -> 121 us
  other arithmetic: 12.4 us -> 16.5 us
    all_gather x0 -> x1, waiting for transfers between devices: none -> 94.9 us  [per_device(): lax.all_gather(partial_memory.astype(jnp.bfloat16), 'sec')]
    psum x1 -> x0, waiting for transfers between devices: 73.1 us -> none  [per_device(): lax.psum(partial_memory.astype(jnp.bfloat16), 'sec').astype(jnp.float32)]
    reduce_sum x0 -> x1, other arithmetic: none -> 5.16 us  [per_device(): jnp.sum(lax.all_gather(partial_memory.astype(jnp.bfloat16), 'sec'), axis=0)]
  transfers between devices with their start and end apart: 6 -> 6, of which waited for: 5 -> 5; matrix products, arithmetic and copies ran while one was open for 45% -> 42% of each run, Pallas kernels for 0% -> 0%
where the time goes in v1:
time: 297 us; the launch traced here: 296 us
  waiting for transfers between devices  121 us (41%)
  local copies, waits for them, and re-layouts  67 us (23%)
  matrix products  64.3 us (22%)
  other arithmetic  16.5 us (6%)
  between operations  14.1 us (5%)
  starting transfers between devices  12.5 us (4%)
    all_gather x1, waiting for transfers between devices, per_device(): lax.all_gather(partial_memory.astype(jnp.bfloat16), 'sec')  94.9 us
    another operation x8, local copies, waits for them, and re-layouts, block_step(): jnp.stack([grad_key, grad_value]).reshape(2, SLOTS, BLOCK, width_here)  27.6 us
    dot_general x2, matrix products, block_step(): jnp.einsum('sj,csrx->cjrx', targets, pair_grads, precision=lax.Precision....  26.7 us
    dot_general x1, matrix products, per_device(): jnp.einsum('crx,cnx->rn', grads_half, lax.all_gather(kv_weight, 'tgt', ax...  12.3 us
    ppermute x2, waiting for transfers between devices, from_behind(): return lax.ppermute(block, axis, route)  11.7 us
    ppermute x1, waiting for transfers between devices, with_halo(): lax.ppermute(lax.slice_in_dim(block, block.shape[dim] - width, None, axis...  9.39 us
    slice x4, local copies, waits for them, and re-layouts, block_step(): value_rows = picked[1].reshape(SLOTS * BLOCK, heads_here, HEAD_DIM)  7.31 us
    while x1, local copies, waits for them, and re-layouts, per_device(): spread_blocks, query_blocks = lax.scan(block_step, start, inputs)  7.02 us
  transfers between devices with their start and end apart: 6, of which 5 were waited for; matrix products, arithmetic and copies ran while one was open for 42% of the time, Pallas kernels for 0%

profile of v1, /device:TPU:1, one launch (start us, length us, event | category | flops | bytes accessed | tf_op | source)
XLA Modules:
  0.0 295.8 jit_solution(6576164579561933458)
XLA Ops:
  7.9 4.9 %collective-permute-start = (bf16[2,256,1024]{2,1,0:T(8,128)(2,1)}, bf16[2,256,1024]{2,1,0:T(8,128)(2,1)S(1)}, u32[]{:S(2)}, u32[]{:S(2)}) collective-permute-start(bf16[2,256,1024]{2,1,0:T(8,128)(2,1)} %param.9), channel_id=1, source_target_pairs={{0,4},{4,8},{8,12},{12,16},{16,20},{20,24},{24,28},{28,32},{32,36}... | collective-permute-start | bytes 3145736 | tf_op jit(solution)/shard_map/ppermute | solution.py:22
  12.9 1.9 collective-permute-start.1
  15.5 9.4 %collective-permute-done = bf16[2,256,1024]{2,1,0:T(8,128)(2,1)S(1)} collective-permute-done((bf16[2,256,1024]{2,1,0:T(8,128)(2,1)}, bf16[2,256,1024]{2,1,0:T(8,128)(2,1)S(1)}, u32[]{:S(2)}, u32[]{:S(2)}) %collective-permute-start) | collective-permute-done | bytes 1048608 | tf_op jit(solution)/shard_map/ppermute | solution.py:22
  24.9 4.3 %collective-permute-done.1 = bf16[2,256,1024]{2,1,0:T(8,128)(2,1)S(1)} collective-permute-done((bf16[2,256,1024]{2,1,0:T(8,128)(2,1)}, bf16[2,256,1024]{2,1,0:T(8,128)(2,1)S(1)}, u32[]{:S(2)}, u32[]{:S(2)}) %collective-permute-start.1) | collective-permute-done | bytes 1048608 | tf_op jit(solution)/shard_map/ppermute | solution.py:25
  29.2 2.8 pad_maximum_fusion
  32.0 116.6 %while.13 = (s32[]{:T(128)}, f32[2,6,128,1024]{3,1,2,0:T(8,128)}, bf16[2,128,1024]{2,1,0:T(8,128)(2,1)}, bf16[2,128,1024]{2,1,0:T(8,128)(2,1)}, s32[2]{0:T(128)S...) while((s32[]{:T(128)}, f32[2,6,128,1024]{3,1,2,0:T(8,128)}, ...), condition=%wide.region_4.5_spmd.clone, body=%wide.region_0.4_spmd.clone.sunk | while | flops 896663104 | bytes 128497184 | solution.py:94
  32.1 2.6 gather_fusion
  34.7 1.2 fusion.87
  39.5 3.4 %fusion.88 = (f32[16,128]{1,0:T(8,128)S(1)}, f32[16,128,512]{2,1,0:T(8,128)}) fusion(pred[512]{0:T(512)(128)(4,1)S(1)} %broadcast_bitcast_fusion.2, bf16[128,16,64]{0,2,1:T(8,128)(2,1)S(1)} %bitcast.126, bf16[512,16,64]{0,2,1:T(8,128)(2,1)S(1)} %squeeze.23), kind=kOutput, calls=%fused_computation.53.clone.1 | convolution fusion | flops 138412544 | bytes 5513728 | tf_op jit(solution)/shard_map/while/body/eval_jaxpr/sub | solution.py:59
  42.8 2.6 fusion.89
  45.4 2.4 copy.38
  47.8 2.3 squeeze.24
  51.2 2.1 fusion.90
  53.4 2.8 multiply_convert_fusion.2
  56.2 1.4 copy-done.1
  57.6 1.8 multiply_bitcast_fusion.2
  59.4 2.9 stack.15
  62.3 3.9 %copy.39 = f32[1,4,128,1024]{3,1,2,0:T(4,128)} copy(f32[1,4,128,1024]{2,1,3,0:T(4,128)} %stack.15) | data formatting | bytes 4194304 | tf_op jit(solution)/shard_map/while/body/eval_jaxpr/stack | solution.py:80
  66.2 1.7 convolution_bitcast_fusion.4
  67.9 2.9 stack.14
  70.8 4.1 %copy.37 = f32[1,4,128,1024]{3,1,2,0:T(4,128)} copy(f32[1,4,128,1024]{2,1,3,0:T(4,128)} %stack.14) | data formatting | bytes 4194304 | tf_op jit(solution)/shard_map/while/body/eval_jaxpr/stack | solution.py:80
  74.9 12.2 %bitcast_add_fusion.2 = f32[2,6,128,1024]{3,1,2,0:T(8,128)} fusion(f32[2,6,128,1024]{3,1,2,0:T(8,128)} %get-tuple-element.185, pred[]{:T(512)S(6)} %compare.3, f32[1,4,128,1024]{3,1,2,0:T(4,128)} %copy.37, f32[1,4,128,1024]{3,1,2,0:T(4,128)S(1)} %copy-done, s32[4]{0:T(128)S(1)} %fusion.91, pred[4]{0:T(512)(128)(4,1)S(1)} %iota_compare_fusion.3), kind=kOutput, calls=%fused_computation.3.clone.1 | convolution fusion | flops 79691824 | bytes 16777236 | tf_op jit(solution)/shard_map/while/body/eval_jaxpr/sj,csrx->cjrx/dot_general | solution.py:82
  89.1 2.7 gather_fusion
  91.8 1.2 fusion.87
  96.6 3.4 %fusion.88 = (f32[16,128]{1,0:T(8,128)S(1)}, f32[16,128,512]{2,1,0:T(8,128)}) fusion(pred[512]{0:T(512)(128)(4,1)S(1)} %broadcast_bitcast_fusion.2, bf16[128,16,64]{0,2,1:T(8,128)(2,1)S(1)} %bitcast.126, bf16[512,16,64]{0,2,1:T(8,128)(2,1)S(1)} %squeeze.23), kind=kOutput, calls=%fused_computation.53.clone.1 | convolution fusion | flops 138412544 | bytes 5513728 | tf_op jit(solution)/shard_map/while/body/eval_jaxpr/sub | solution.py:59
  100.0 2.6 fusion.89
  102.6 2.4 copy.38
  105.1 2.3 squeeze.24
  107.3 1.1 copy.34
  108.4 2.1 fusion.90
  110.6 2.9 multiply_convert_fusion.2
  113.6 1.4 copy-done.1
  115.0 1.8 multiply_bitcast_fusion.2
  116.7 2.9 stack.15
  119.6 3.9 %copy.39 = f32[1,4,128,1024]{3,1,2,0:T(4,128)} copy(f32[1,4,128,1024]{2,1,3,0:T(4,128)} %stack.15) | data formatting | bytes 4194304 | tf_op jit(solution)/shard_map/while/body/eval_jaxpr/stack | solution.py:80
  123.5 1.7 convolution_bitcast_fusion.4
  125.3 2.9 stack.14
  128.2 4.1 %copy.37 = f32[1,4,128,1024]{3,1,2,0:T(4,128)} copy(f32[1,4,128,1024]{2,1,3,0:T(4,128)} %stack.14) | data formatting | bytes 4194304 | tf_op jit(solution)/shard_map/while/body/eval_jaxpr/stack | solution.py:80
  132.3 14.5 %bitcast_add_fusion.2 = f32[2,6,128,1024]{3,1,2,0:T(8,128)} fusion(f32[2,6,128,1024]{3,1,2,0:T(8,128)} %get-tuple-element.185, pred[]{:T(512)S(6)} %compare.3, f32[1,4,128,1024]{3,1,2,0:T(4,128)} %copy.37, f32[1,4,128,1024]{3,1,2,0:T(4,128)S(1)} %copy-done, s32[4]{0:T(128)S(1)} %fusion.91, pred[4]{0:T(512)(128)(4,1)S(1)} %iota_compare_fusion.3), kind=kOutput, calls=%fused_computation.3.clone.1 | convolution fusion | flops 79691824 | bytes 16777236 | tf_op jit(solution)/shard_map/while/body/eval_jaxpr/sj,csrx->cjrx/dot_general | solution.py:82
  148.6 7.0 %copy.20 = f32[2,6,128,1024]{3,2,1,0:T(8,128)S(1)} copy(f32[2,6,128,1024]{3,1,2,0:T(8,128)} %get-tuple-element.51) | data formatting | bytes 12582912 | tf_op jit(solution)/shard_map/while | solution.py:94
  156.1 2.2 copy-done.6
  158.5 1.9 collective-permute-start.2
  160.4 3.6 %collective-permute-start.3 = (bf16[2,256,1024]{2,1,0:T(8,128)(2,1)S(1)}, bf16[2,256,1024]{2,1,0:T(8,128)(2,1)S(1)}, u32[]{:S(2)}, u32[]{:S(2)}) collective-permute-start(bf16[2,256,1024]{2,1,0:T(8,128)(2,1)S(1)} %get-tuple-element.112), channel_id=1, source_target_pairs={{0,4},{4,8},{8,12},{12,16},{16,20},{20,24},{24,28},{28,32},{32,36}... | collective-permute-start | bytes 3145736 | tf_op jit(solution)/shard_map/ppermute | solution.py:14
  164.0 10.5 %collective-permute-done.2 = bf16[2,256,1024]{2,1,0:T(8,128)(2,1)S(1)} collective-permute-done((bf16[2,256,1024]{2,1,0:T(8,128)(2,1)S(1)}, bf16[2,256,1024]{2,1,0:T(8,128)(2,1)S(1)}, u32[]{:S(2)}, u32[]{:S(2)}) %collective-permute-start.2) | collective-permute-done | bytes 1048608 | tf_op jit(solution)/shard_map/ppermute | solution.py:14
  174.6 1.2 collective-permute-done.3
  175.8 12.3 %fusion.29 = bf16[256,4096]{1,0:T(8,128)(2,1)} fusion(bf16[2,4096,1024]{2,1,0:T(8,128)(2,1)} %all-gather.4.cloned.1.call-done, f32[2,768,1024]{2,1,0:T(8,128)} %bitcast.129, bf16[2,256,1024]{2,1,0:T(8,128)(2,1)S(1)} %collective-permute-done.3, bf16[2,256,1024]{2,1,0:T(8,128)(2,1)S(1)} %collective-permute-done.2), kind=kOutput, calls=%fused_computation.44 | convolution fusion | flops 4298637312 | bytes 23068672 | tf_op jit(solution)/shard_map/crx,cnx->rn/dot_general | solution.py:101
  188.1 94.9 %all-gather.6.cloned.1.call-done = bf16[1024,4096]{1,0:T(8,128)(2,1)} async-done(((bf16[256,4096]{1,0:T(8,128)(2,1)}), bf16[1024,4096]{1,0:T(8,128)(2,1)}) %all-gather.6.cloned.1.call-update) | async-done | bytes 8388624 | tf_op jit(solution)/shard_map/all_gather | solution.py:108
  283.0 5.2 %reduce_sum.30 = bf16[256,4096]{1,0:T(8,128)(2,1)S(1)} reduce(bf16[4,256,4096]{2,1,0:T(8,128)(2,1)} %bitcast.130, bf16[]{:T(256)} %constant.12.clone.1), dimensions={0}, to_apply=%region_5.6 | reduce | flops 3145728 | bytes 10485762 | tf_op jit(solution)/shard_map/reduce_sum | solution.py:107
  (79 shorter events, 14.9 us)
Async XLA Ops:
  7.2 168.6 %all-gather.4.cloned.1.call-start = ((), (), s32[]{:S(2)}) async-start(), calls=%async_computation | async-start | bytes 17039360 | tf_op jit(solution)/shard_map/all_gather | solution.py:104
  7.9 275.1 %all-gather.6.cloned.1.call-start = ((), (), s32[]{:S(2)}) async-start(), calls=%async_computation.1 | async-start | bytes 10485760 | tf_op jit(solution)/shard_map/all_gather | solution.py:108
  7.9 17.0 %collective-permute-start = (bf16[2,256,1024]{2,1,0:T(8,128)(2,1)}, bf16[2,256,1024]{2,1,0:T(8,128)(2,1)S(1)}, u32[]{:S(2)}, u32[]{:S(2)}) collective-permute-start(bf16[2,256,1024]{2,1,0:T(8,128)(2,1)} %param.9), channel_id=1, source_target_pairs={{0,4},{4,8},{8,12},{12,16},{16,20},{20,24},{24,28},{28,32},{32,36}... | collective-permute-start | bytes 3145736 | tf_op jit(solution)/shard_map/ppermute | solution.py:22
  12.9 16.3 %collective-permute-start.1 = (bf16[2,256,1024]{2,1,0:T(8,128)(2,1)}, bf16[2,256,1024]{2,1,0:T(8,128)(2,1)S(1)}, u32[]{:S(2)}, u32[]{:S(2)}) collective-permute-start(bf16[2,256,1024]{2,1,0:T(8,128)(2,1)} %param.9), channel_id=1, source_target_pairs={{4,0},{8,4},{12,8},{16,12},{20,16},{24,20},{28,24},{32,28},{36,32}... | collective-permute-start | bytes 3145736 | tf_op jit(solution)/shard_map/ppermute | solution.py:25
  15.5 16.5 %copy-start.11 = (s32[2]{0:T(128)S(1)}, s32[2]{0:T(128)}, u32[]{:S(2)}) copy-start(s32[2]{0:T(128)} %param.12) | copy-start | bytes 28
  35.9 1.2 copy-start.7
  35.9 1.2 copy-start.8
  38.1 4.8 %copy-start.4 = (bf16[1,128,1024]{1,2,0:T(8,128)(2,1)}, bf16[1,128,1024]{1,2,0:T(8,128)(2,1)S(1)}, u32[]{:S(2)}) copy-start(bf16[1,128,1024]{1,2,0:T(8,128)(2,1)S(1)} %copy.35) | copy-start | bytes 786436 | tf_op jit(solution)/shard_map/while
  51.2 2.2 copy-start.3
  53.4 4.2 %copy-start.5 = (bf16[1,128,1024]{1,2,0:T(8,128)(2,1)S(1)}, bf16[1,128,1024]{1,2,0:T(8,128)(2,1)}, u32[]{:S(2)}) copy-start(bf16[1,128,1024]{1,2,0:T(8,128)(2,1)} %copy-done.4) | copy-start | bytes 786436 | tf_op jit(solution)/shard_map/while
  56.2 1.4 copy-start.1
  70.8 4.1 %copy-start = (f32[1,4,128,1024]{3,1,2,0:T(4,128)S(1)}, f32[1,4,128,1024]{3,1,2,0:T(4,128)}, u32[]{:S(2)}) copy-start(f32[1,4,128,1024]{3,1,2,0:T(4,128)} %copy.39) | copy-start | bytes 6291460 | tf_op jit(solution)/shard_map/while
  74.9 12.2 %copy-start.2 = (bf16[16,128,512]{2,1,0:T(8,128)(2,1)S(1)}, bf16[16,128,512]{2,1,0:T(8,128)(2,1)}, u32[]{:S(2)}) copy-start(bf16[16,128,512]{2,1,0:T(8,128)(2,1)} %copy-done.1) | copy-start | bytes 6291460 | tf_op jit(solution)/shard_map/while
  87.1 1.2 copy-start.9
  88.3 0.8 copy-start.10
  93.1 1.2 copy-start.7
  93.1 1.2 copy-start.8
  95.2 4.8 %copy-start.4 = (bf16[1,128,1024]{1,2,0:T(8,128)(2,1)}, bf16[1,128,1024]{1,2,0:T(8,128)(2,1)S(1)}, u32[]{:S(2)}) copy-start(bf16[1,128,1024]{1,2,0:T(8,128)(2,1)S(1)} %copy.35) | copy-start | bytes 786436 | tf_op jit(solution)/shard_map/while
  108.4 2.2 copy-start.3
  110.6 4.3 %copy-start.5 = (bf16[1,128,1024]{1,2,0:T(8,128)(2,1)S(1)}, bf16[1,128,1024]{1,2,0:T(8,128)(2,1)}, u32[]{:S(2)}) copy-start(bf16[1,128,1024]{1,2,0:T(8,128)(2,1)} %copy-done.4) | copy-start | bytes 786436 | tf_op jit(solution)/shard_map/while
  113.6 1.4 copy-start.1
  128.2 4.1 %copy-start = (f32[1,4,128,1024]{3,1,2,0:T(4,128)S(1)}, f32[1,4,128,1024]{3,1,2,0:T(4,128)}, u32[]{:S(2)}) copy-start(f32[1,4,128,1024]{3,1,2,0:T(4,128)} %copy.39) | copy-start | bytes 6291460 | tf_op jit(solution)/shard_map/while
  132.2 14.5 %copy-start.2 = (bf16[16,128,512]{2,1,0:T(8,128)(2,1)S(1)}, bf16[16,128,512]{2,1,0:T(8,128)(2,1)}, u32[]{:S(2)}) copy-start(bf16[16,128,512]{2,1,0:T(8,128)(2,1)} %copy-done.1) | copy-start | bytes 6291460 | tf_op jit(solution)/shard_map/while
  146.7 1.0 copy-start.9
  147.8 0.8 copy-start.10
  155.6 2.7 copy-start.6
  158.5 16.1 %collective-permute-start.2 = (bf16[2,256,1024]{2,1,0:T(8,128)(2,1)S(1)}, bf16[2,256,1024]{2,1,0:T(8,128)(2,1)S(1)}, u32[]{:S(2)}, u32[]{:S(2)}) collective-permute-start(bf16[2,256,1024]{2,1,0:T(8,128)(2,1)S(1)} %get-tuple-element.111), channel_id=1, source_target_pairs={{4,0},{8,4},{12,8},{16,12},{20,16},{24,20},{28,24},{32,28},{36,32}... | collective-permute-start | bytes 3145736 | tf_op jit(solution)/shard_map/ppermute | solution.py:14
  160.4 15.4 %collective-permute-start.3 = (bf16[2,256,1024]{2,1,0:T(8,128)(2,1)S(1)}, bf16[2,256,1024]{2,1,0:T(8,128)(2,1)S(1)}, u32[]{:S(2)}, u32[]{:S(2)}) collective-permute-start(bf16[2,256,1024]{2,1,0:T(8,128)(2,1)S(1)} %get-tuple-element.112), channel_id=1, source_target_pairs={{0,4},{4,8},{8,12},{12,16},{16,20},{20,24},{24,28},{28,32},{32,36}... | collective-permute-start | bytes 3145736 | tf_op jit(solution)/shard_map/ppermute | solution.py:14
Sparse Core Ops, SparseCore 0:
  10.8 104.2 all-gather.3
  188.2 94.7 all-gather.5
